TPU v7x, 512 devices: a whole 4x8x8 slice. The times are simulated.
512 devices in a mesh: dp: 32 (over x, z), tensor: 16 (over y, core).
Axes of the slice: x: 4, y: 8, z: 8, core: 2. Of those that a mesh axis runs over, the one named last changes fastest.
Arguments:
- tokens: bfloat16 [8192, 4096], P('dp', 'tensor'), may hold values from -6 to 6
- out_grad: bfloat16 [8192, 4096], P('dp', 'tensor'), may hold values from -0.59765625 to 0.59765625
- w_in: bfloat16 [384, 128, 128], P('tensor'), may hold values from -0.25 to 0.25
- w_out: bfloat16 [384, 128, 128], P('tensor'), may hold values from -0.25 to 0.25
- block_rows: int32 [16, 24], P('tensor'), may hold values from -1 to 31, as said below
- block_cols: int32 [16, 24], P('tensor'), may hold values from -1 to 6, as said below
Outputs:
- in_grad: bfloat16 [8192, 4096], P('dp')
- win_grad: float32 [384, 16384], P('tensor', 'dp')
- wout_grad: float32 [384, 16384], P('tensor', 'dp')
Inputs may be any that keep to these rules, and one draw needn't show every extreme that they name: `block_rows`: -1 marks an empty slot; the live slots of one tensor index name distinct blocks; at least 12 slots of each tensor index are live, and all 24 slots of some tensor index are live. `block_cols`: -1 exactly where block_rows is -1.
All inputs are finite; a program needn't handle non-finite values.
Results may differ from a plain program's by a relative error of at most 0.02.
Values may be sent and summed in bfloat16 or wider, within the bound.
No kernel may reach another device: no remote copies, remote signals or barrier semaphores. Data moves between devices by JAX's collectives and lax.ppermute only.
A program may use at most 64 MiB of HBM per device.

v0:
```python
import jax
import jax.numpy as jnp
from jax import lax
from jax.sharding import PartitionSpec as P

FF = 14336
highest = lax.Precision.HIGHEST
clip_limit = 4.0


def local(tokens, out_grad, w_in, w_out, block_rows, block_cols):
    bin_scale = 4194304.0 / lax.axis_size("dp")
    whole_tokens, whole_grad = (
        lax.all_gather(tokens, "tensor", axis=1, tiled=True),
        lax.all_gather(out_grad, "tensor", axis=1, tiled=True),
    )
    tok_count = whole_tokens.shape[0]
    width = whole_tokens.shape[1]
    side = w_in.shape[1]
    row_count = width // side
    col_count = FF // side // lax.axis_size("tensor")
    rows = block_rows[0]
    cols = block_cols[0]
    live = rows >= 0
    livef = live.astype(jnp.float32)
    safe_rows = jnp.where(live, rows, 0)
    safe_cols = jnp.where(live, cols, 0)
    col_hot = (safe_cols[:, None] == jnp.arange(col_count, dtype=jnp.int32)[None, :]).astype(
        jnp.float32
    ) * livef[:, None]
    row_hot = (safe_rows[:, None] == jnp.arange(row_count, dtype=jnp.int32)[None, :]).astype(
        jnp.float32
    ) * livef[:, None]
    in_blocks = whole_tokens.reshape(tok_count, row_count, side).transpose(1, 0, 2)
    grad_blocks = whole_grad.reshape(tok_count, row_count, side).transpose(1, 0, 2)
    picked = jnp.take(in_blocks, safe_rows, axis=0)
    picked_grad = jnp.take(grad_blocks, safe_rows, axis=0)
    slot_pre = jnp.einsum("stk,skh->sth", picked, w_in, preferred_element_type=jnp.float32)
    pre = jnp.einsum("sc,sth->cth", col_hot, slot_pre, precision=highest)
    hidden = jax.nn.silu(pre).astype(jnp.bfloat16)
    slot_back = jnp.einsum("std,shd->sth", picked_grad, w_out, preferred_element_type=jnp.float32)
    dhidden = jnp.einsum("sc,sth->cth", col_hot, slot_back, precision=highest)
    sigma = jax.nn.sigmoid(pre)
    dpre = (dhidden * sigma * (1.0 + pre * (1.0 - sigma))).astype(jnp.bfloat16)
    dpre_picked = jnp.take(dpre, safe_cols, axis=0)
    hidden_picked = jnp.take(hidden, safe_cols, axis=0)
    slot_terms = jnp.einsum("sth,sdh->std", dpre_picked, w_in, preferred_element_type=jnp.float32)
    partial_grad = jnp.einsum("sr,std->rtd", row_hot, slot_terms, precision=highest)
    summed = lax.psum(partial_grad.astype(jnp.bfloat16), "tensor")
    in_grad = summed.transpose(1, 0, 2).reshape(tok_count, width)
    grad_in = (
        jnp.einsum("stk,sth->skh", picked, dpre_picked, preferred_element_type=jnp.float32)
        * livef[:, None, None]
    )
    grad_out = (
        jnp.einsum("sth,std->shd", hidden_picked, picked_grad, preferred_element_type=jnp.float32)
        * livef[:, None, None]
    )
    slot_count = grad_in.shape[0]
    bins_in = jnp.floor(jnp.clip(grad_in, -clip_limit, clip_limit) * bin_scale).reshape(
        slot_count, side * side
    )
    bins_out = jnp.floor(jnp.clip(grad_out, -clip_limit, clip_limit) * bin_scale).reshape(
        slot_count, side * side
    )
    total_in, total_out = (
        lax.psum_scatter(
            bins_in.astype(jnp.bfloat16), "dp", scatter_dimension=1, tiled=True
        ).astype(jnp.float32),
        lax.psum_scatter(
            bins_out.astype(jnp.bfloat16), "dp", scatter_dimension=1, tiled=True
        ).astype(jnp.float32),
    )
    win_grad = total_in / bin_scale
    wout_grad = total_out / bin_scale
    return (in_grad, win_grad, wout_grad)


def solution(mesh):
    in_specs = (
        P("dp", "tensor"),
        P("dp", "tensor"),
        P("tensor", None, None),
        P("tensor", None, None),
        P("tensor", None),
        P("tensor", None),
    )
    out_specs = (P("dp", None), P("tensor", "dp"), P("tensor", "dp"))
    return jax.shard_map(local, mesh=mesh, in_specs=in_specs, out_specs=out_specs, check_vma=False)
```

profile of v0, /device:TPU:1, one launch (start us, length us, event | category | flops | bytes accessed | tf_op | source)
XLA Modules:
  0.0 698.1 jit_solution(12155008888850396349)
XLA Ops:
  7.2 1.7 copy.18
  9.0 1.7 copy.15
  10.7 0.0 reduce-scatter.3.cloned.1.call-start
  10.8 0.7 compare_and_fusion
  11.5 46.5 %all-gather.5.cloned.1.call-done = bf16[256,4096]{0,1:T(8,128)(2,1)} async-done(((bf16[256,256]{0,1:T(8,128)(2,1)}), bf16[256,4096]{0,1:T(8,128)(2,1)}) %all-gather.5.cloned.1.call-update) | async-done | bytes 2097168 | tf_op jit(solution)/shard_map/all_gather | solution.py:14
  58.0 3.2 copy.19
  61.2 40.3 %all-gather.3.cloned.1.call-done = bf16[256,4096]{0,1:T(8,128)(2,1)} async-done(((bf16[256,256]{0,1:T(8,128)(2,1)}), bf16[256,4096]{0,1:T(8,128)(2,1)}) %all-gather.3.cloned.1.call-update) | async-done | bytes 2097168 | tf_op jit(solution)/shard_map/all_gather | solution.py:15
  101.5 4.1 copy.16
  105.6 1.9 gather_fusion.1
  107.5 2.4 gather_fusion
  110.0 2.6 fusion.25
  112.6 3.6 multiply_convert_fusion
  116.2 0.6 fusion.24
  116.8 3.7 fusion.20
  120.6 0.1 copy.21
  120.6 0.8 gather_fusion.2
  121.5 2.3 floor_convert_fusion.1
  123.8 1.4 copy.52
  125.3 0.2 reduce-scatter.5.cloned.1.call-start
  125.5 0.1 copy.24
  125.6 1.9 gather_fusion.3
  127.5 2.8 floor_convert_fusion
  130.3 1.4 copy.51
  131.8 0.6 fusion.26
  132.5 6.7 fusion.6
  139.2 2.3 copy.50
  141.5 198.4 %reduce-scatter.3.cloned.1.call-done = bf16[24,512]{1,0:T(8,128)(2,1)} async-done(((bf16[24,16384]{1,0:T(8,128)(2,1)}), bf16[24,512]{1,0:T(8,128)(2,1)}) %reduce-scatter.3.cloned.1.call-update) | async-done | bytes 24592 | tf_op jit(solution)/shard_map/reduce_scatter | solution.py:67
  339.9 1.4 convert_multiply_fusion.1
  341.2 221.7 %reduce-scatter.5.cloned.1.call-done = bf16[24,512]{1,0:T(8,128)(2,1)} async-done(((bf16[24,16384]{1,0:T(8,128)(2,1)}), bf16[24,512]{1,0:T(8,128)(2,1)}) %reduce-scatter.5.cloned.1.call-update) | async-done | bytes 24592 | tf_op jit(solution)/shard_map/reduce_scatter | solution.py:70
  562.9 1.4 convert_multiply_fusion
  564.3 124.2 %all-reduce.2.cloned.1.call-done = bf16[256,4096]{1,0:T(8,128)(2,1)} async-done(((bf16[256,4096]{1,0:T(8,128)(2,1)}), bf16[256,4096]{1,0:T(8,128)(2,1)}) %all-reduce.2.cloned.1.call-update) | async-done | bytes 2097168 | tf_op jit(solution)/shard_map/psum | solution.py:49
  688.4 3.1 copy.54
  (20 shorter events, 0.2 us)
Async XLA Ops:
  7.2 102.8 %copy-start = (bf16[24,128,128]{2,1,0:T(8,128)(2,1)S(1)}, bf16[24,128,128]{2,1,0:T(8,128)(2,1)}, u32[]{:S(2)}) copy-start(bf16[24,128,128]{2,1,0:T(8,128)(2,1)} %param.12) | copy-start | bytes 2359300
  7.2 50.8 %all-gather.5.cloned.1.call-start = ((), (), s32[]{:S(2)}) async-start(), calls=%async_computation.3 | async-start | bytes 2228224 | tf_op jit(solution)/shard_map/all_gather | solution.py:14
  9.0 92.5 %all-gather.3.cloned.1.call-start = ((), (), s32[]{:S(2)}) async-start(), calls=%async_computation.2 | async-start | bytes 2228224 | tf_op jit(solution)/shard_map/all_gather | solution.py:15
  10.7 329.2 %reduce-scatter.3.cloned.1.call-start = ((), (), s32[]{:S(2)}) async-start(), calls=%async_computation.5 | async-start | bytes 811008 | tf_op jit(solution)/shard_map/reduce_scatter | solution.py:67
  110.0 6.2 copy-start.1
  112.6 3.6 copy-start.2
  125.3 437.6 %reduce-scatter.5.cloned.1.call-start = ((), (), s32[]{:S(2)}) async-start(), calls=%async_computation.6 | async-start | bytes 811008 | tf_op jit(solution)/shard_map/reduce_scatter | solution.py:70
  130.3 1.5 copy-start.3
  131.8 556.7 %all-reduce.2.cloned.1.call-start = ((), (), s32[]{:S(2)}) async-start(), calls=%async_computation.4 | async-start | bytes 4194304 | tf_op jit(solution)/shard_map/psum | solution.py:49
Sparse Core Ops, SparseCore 0:
  10.1 47.7 all-gather.4
  60.7 40.7 all-gather.2
  125.4 214.4 reduce-scatter.2
  344.1 218.7 reduce-scatter.4
  565.7 122.7 all-reduce.1
where the time goes:
time: 699 us; the launch traced here: 698 us
  waiting for transfers between devices  631 us (90%)
  local copies, waits for them, and re-layouts  26.2 us (4%)
  matrix products  23 us (3%)
  between operations  14 us (2%)
    reduce_scatter x1, waiting for transfers between devices, local(): lax.psum_scatter(bins_out.astype(jnp.bfloat16), 'dp', scatter_dimension=1...  222 us
    reduce_scatter x1, waiting for transfers between devices, local(): lax.psum_scatter(bins_in.astype(jnp.bfloat16), 'dp', scatter_dimension=1,...  198 us
    psum x1, waiting for transfers between devices, local(): summed = lax.psum(partial_grad.astype(jnp.bfloat16), 'tensor')  124 us
    all_gather x1, waiting for transfers between devices, local(): lax.all_gather(tokens, 'tensor', axis=1, tiled=True)  46.5 us
    all_gather x1, waiting for transfers between devices, local(): lax.all_gather(out_grad, 'tensor', axis=1, tiled=True)  40.3 us
  transfers between devices with their start and end apart: 5, of which 5 were waited for; matrix products, arithmetic and copies ran while one was open for 3% of the time, Pallas kernels for 0%

commit v1 on v0

--- a/solution.py
+++ b/solution.py
@@ -2,16 +2,32 @@
 import jax.numpy as jnp
 from jax import lax
 from jax.sharding import PartitionSpec as P
+from jax.lax import axis_index, axis_size, ppermute
 
 FF = 14336
 highest = lax.Precision.HIGHEST
 clip_limit = 4.0
 
 
+def cover_tables(message):
+    n_axis = axis_size("tensor")
+    all_rows = [(to_i, (to_i + 1) % n_axis) for to_i in range(n_axis)]
+    items = [(to_i, (to_i - 1) % n_axis) for to_i in range(n_axis)]
+    e_next, clean = ([message], [message])
+    for _ in range(n_axis // 2):
+        e_next.append(ppermute(e_next[-1], "tensor", all_rows))
+    q = 0
+    while q < (n_axis - 1) // 2:
+        clean.append(ppermute(clean[-1], "tensor", items))
+        q = q + 1
+    raw_out = jnp.concatenate([*e_next[::-1], *clean[1:]], 1)
+    return jnp.roll(raw_out, (axis_index("tensor") - n_axis // 2) * message.shape[1], 1)
+
+
 def local(tokens, out_grad, w_in, w_out, block_rows, block_cols):
     bin_scale = 4194304.0 / lax.axis_size("dp")
     whole_tokens, whole_grad = (
-        lax.all_gather(tokens, "tensor", axis=1, tiled=True),
+        cover_tables(tokens),
         lax.all_gather(out_grad, "tensor", axis=1, tiled=True),
     )
     tok_count = whole_tokens.shape[0]

time: 699 us -> 676 us (0.967)
  waiting for transfers between devices: 631 us -> 574 us
  starting transfers between devices: 0.39 us -> 35.6 us
    all_gather x1 -> x0, waiting for transfers between devices: 46.5 us -> none  [local(): lax.all_gather(tokens, 'tensor', axis=1, tiled=True)]
    ppermute x0 -> x15, starting transfers between devices: none -> 35.2 us  [the longest x7 32.5 us: cover_tables(): clean.append(ppermute(clean[-1], 'tensor', items))]
    all_gather x1, waiting for transfers between devices: 40.3 us -> 18.4 us  [local(): lax.all_gather(out_grad, 'tensor', axis=1, tiled=True)]
    ppermute x0 -> x15, waiting for transfers between devices: none -> 10.8 us  [the longest x8 8.38 us: cover_tables(): e_next.append(ppermute(e_next[-1], 'tensor', all_rows))]
  transfers between devices with their start and end apart: 5 -> 19, of which waited for: 5 -> 15; matrix products, arithmetic and copies ran while one was open for 3% -> 5% of each run, Pallas kernels for 0% -> 0%
where the time goes in v1:
time: 676 us; the launch traced here: 675 us
  waiting for transfers between devices  574 us (85%)
  starting transfers between devices  35.6 us (5%)
  local copies, waits for them, and re-layouts  24.8 us (4%)
  matrix products  23.6 us (3%)
  between operations  14.2 us (2%)
    reduce_scatter x1, waiting for transfers between devices, local(): lax.psum_scatter(bins_out.astype(jnp.bfloat16), 'dp', scatter_dimension=1...  222 us
    reduce_scatter x1, waiting for transfers between devices, local(): lax.psum_scatter(bins_in.astype(jnp.bfloat16), 'dp', scatter_dimension=1,...  199 us
    psum x1, waiting for transfers between devices, local(): summed = lax.psum(partial_grad.astype(jnp.bfloat16), 'tensor')  124 us
    ppermute x7, starting transfers between devices, cover_tables(): clean.append(ppermute(clean[-1], 'tensor', items))  32.5 us
    all_gather x1, waiting for transfers between devices, local(): lax.all_gather(out_grad, 'tensor', axis=1, tiled=True)  18.4 us
  transfers between devices with their start and end apart: 19, of which 15 were waited for; matrix products, arithmetic and copies ran while one was open for 5% of the time, Pallas kernels for 0%

profile of v1, /device:TPU:1, one launch (start us, length us, event | category | flops | bytes accessed | tf_op | source)
XLA Modules:
  0.0 675.3 jit_solution(1077240285103685817)
XLA Ops:
  7.2 1.1 copy.18
  8.3 2.7 collective-permute-start
  11.0 5.0 collective-permute-done
  16.0 4.8 collective-permute-start.8
  21.8 4.6 collective-permute-start.9
  27.4 4.6 collective-permute-start.10
  33.0 4.6 collective-permute-start.11
  38.5 1.6 copy.15
  40.2 4.8 collective-permute-start.12
  45.9 4.5 collective-permute-start.13
  51.4 4.6 collective-permute-start.14
  57.5 2.9 copy.22
  60.4 2.4 gather_fusion.1
  63.4 4.5 multiply_convert_fusion
  67.9 18.4 %all-gather.2.cloned.1.call-done = bf16[256,4096]{0,1:T(8,128)(2,1)} async-done(((bf16[256,256]{0,1:T(8,128)(2,1)}), bf16[256,4096]{0,1:T(8,128)(2,1)}) %all-gather.2.cloned.1.call-update) | async-done | bytes 2097168 | tf_op jit(solution)/shard_map/all_gather | solution.py:31
  86.3 3.2 copy.16
  89.5 1.9 gather_fusion
  91.5 2.3 fusion.24
  93.8 3.7 fusion.20
  98.4 2.3 floor_convert_fusion.1
  100.8 1.4 copy.55
  102.5 2.0 gather_fusion.3
  104.5 2.8 floor_convert_fusion
  107.3 1.4 copy.54
  109.4 6.7 fusion.6
  116.1 2.3 copy.53
  118.4 198.6 %reduce-scatter.3.cloned.1.call-done = bf16[24,512]{1,0:T(8,128)(2,1)} async-done(((bf16[24,16384]{1,0:T(8,128)(2,1)}), bf16[24,512]{1,0:T(8,128)(2,1)}) %reduce-scatter.3.cloned.1.call-update) | async-done | bytes 24592 | tf_op jit(solution)/shard_map/reduce_scatter | solution.py:83
  317.0 1.4 convert_multiply_fusion.1
  318.3 221.8 %reduce-scatter.5.cloned.1.call-done = bf16[24,512]{1,0:T(8,128)(2,1)} async-done(((bf16[24,16384]{1,0:T(8,128)(2,1)}), bf16[24,512]{1,0:T(8,128)(2,1)}) %reduce-scatter.5.cloned.1.call-update) | async-done | bytes 24592 | tf_op jit(solution)/shard_map/reduce_scatter | solution.py:86
  540.2 1.4 convert_multiply_fusion
  541.5 124.1 %all-reduce.2.cloned.1.call-done = bf16[256,4096]{1,0:T(8,128)(2,1)} async-done(((bf16[256,4096]{1,0:T(8,128)(2,1)}), bf16[256,4096]{1,0:T(8,128)(2,1)}) %all-reduce.2.cloned.1.call-update) | async-done | bytes 2097168 | tf_op jit(solution)/shard_map/psum | solution.py:65
  665.6 3.1 copy.88
  (79 shorter events, 9.6 us)
Async XLA Ops:
  7.2 55.6 %copy-start = (bf16[24,128,128]{2,1,0:T(8,128)(2,1)S(1)}, bf16[24,128,128]{2,1,0:T(8,128)(2,1)}, u32[]{:S(2)}) copy-start(bf16[24,128,128]{2,1,0:T(8,128)(2,1)} %param.12) | copy-start | bytes 2359300
  7.2 79.1 %all-gather.2.cloned.1.call-start = ((), (), s32[]{:S(2)}) async-start(), calls=%async_computation.2 | async-start | bytes 2228224 | tf_op jit(solution)/shard_map/all_gather | solution.py:31
  8.3 7.7 %collective-permute-start = (bf16[256,256]{0,1:T(8,128)(2,1)S(1)}, bf16[256,256]{0,1:T(8,128)(2,1)S(1)}, u32[]{:S(2)}, u32[]{:S(2)}) collective-permute-start(bf16[256,256]{0,1:T(8,128)(2,1)S(1)} %copy.18), channel_id=1, source_target_pairs={{0,1},{1,2},{2,3},{3,4},{4,5},{5,6},{6,7},{7,8},{8,9},{9,10},{10,1... | collective-permute-start | bytes 393224 | tf_op jit(solution)/shard_map/ppermute | solution.py:18
  16.0 5.6 collective-permute-start.1
  16.0 5.7 collective-permute-start.8
  21.6 5.6 collective-permute-start.2
  21.8 5.6 collective-permute-start.9
  27.2 5.6 collective-permute-start.3
  27.4 5.6 collective-permute-start.10
  32.8 5.6 collective-permute-start.4
  33.0 7.2 %collective-permute-start.11 = (bf16[256,256]{0,1:T(8,128)(2,1)S(1)}, bf16[256,256]{0,1:T(8,128)(2,1)S(1)}, u32[]{:S(2)}, u32[]{:S(2)}) collective-permute-start(bf16[256,256]{0,1:T(8,128)(2,1)S(1)} %collective-permute-done.10), channel_id=1, source_target_pairs={{0,15},{1,0},{2,1},{3,2},{4,3},{5,4},{6,5},{7,6},{8,7},{9,8},{10,9... | collective-permute-start | bytes 393224 | tf_op jit(solution)/shard_map/ppermute | solution.py:21
  38.4 6.5 collective-permute-start.5
  40.1 276.9 %reduce-scatter.3.cloned.1.call-start = ((), (), s32[]{:S(2)}) async-start(), calls=%async_computation.4 | async-start | bytes 811008 | tf_op jit(solution)/shard_map/reduce_scatter | solution.py:83
  40.2 5.8 collective-permute-start.12
  45.0 5.5 collective-permute-start.6
  45.9 5.5 collective-permute-start.13
  50.4 5.6 collective-permute-start.7
  51.4 5.6 collective-permute-start.14
  62.8 5.1 copy-start.1
  91.5 2.3 copy-start.3
  102.2 438.0 %reduce-scatter.5.cloned.1.call-start = ((), (), s32[]{:S(2)}) async-start(), calls=%async_computation.5 | async-start | bytes 811008 | tf_op jit(solution)/shard_map/reduce_scatter | solution.py:86
  104.5 4.3 copy-start.2
  108.7 556.9 %all-reduce.2.cloned.1.call-start = ((), (), s32[]{:S(2)}) async-start(), calls=%async_computation.3 | async-start | bytes 4194304 | tf_op jit(solution)/shard_map/psum | solution.py:65
Sparse Core Ops, SparseCore 0:
  40.2 46.0 all-gather.1
  102.3 214.6 reduce-scatter.2
  321.4 218.7 reduce-scatter.4
  543.0 122.6 all-reduce.1

commit v2 on v0

--- a/solution.py
+++ b/solution.py
@@ -46,7 +46,8 @@
     hidden_picked = jnp.take(hidden, safe_cols, axis=0)
     slot_terms = jnp.einsum("sth,sdh->std", dpre_picked, w_in, preferred_element_type=jnp.float32)
     partial_grad = jnp.einsum("sr,std->rtd", row_hot, slot_terms, precision=highest)
-    summed = lax.psum(partial_grad.astype(jnp.bfloat16), "tensor")
+    set_area = lambda mine, across: jnp.sum(lax.all_gather(mine, across), axis=0)
+    summed = set_area(partial_grad.astype(jnp.bfloat16), "tensor")
     in_grad = summed.transpose(1, 0, 2).reshape(tok_count, width)
     grad_in = (
         jnp.einsum("stk,sth->skh", picked, dpre_picked, preferred_element_type=jnp.float32)

time: 699 us -> 766 us (1.096)
  waiting for transfers between devices: 631 us -> 690 us
  other arithmetic: 3.43 us -> 15 us
    all_gather x0 -> x1, waiting for transfers between devices: none -> 181 us  [local(): lax.all_gather(mine, across)]
    psum x1 -> x0, waiting for transfers between devices: 124 us -> none  [local(): summed = lax.psum(partial_grad.astype(jnp.bfloat16), 'tensor')]
    reduce_sum x0 -> x1, other arithmetic: none -> 11.6 us  [local(): jnp.sum(lax.all_gather(mine, across), axis=0)]
where the time goes in v2:
time: 766 us; the launch traced here: 765 us
  waiting for transfers between devices  690 us (90%)
  local copies, waits for them, and re-layouts  24.5 us (3%)
  matrix products  22 us (3%)
  other arithmetic  15 us (2%)
  between operations  14 us (2%)
    reduce_scatter x1, waiting for transfers between devices, local(): lax.psum_scatter(bins_out.astype(jnp.bfloat16), 'dp', scatter_dimension=1...  222 us
    reduce_scatter x1, waiting for transfers between devices, local(): lax.psum_scatter(bins_in.astype(jnp.bfloat16), 'dp', scatter_dimension=1,...  200 us
    all_gather x1, waiting for transfers between devices, local(): lax.all_gather(mine, across)  181 us
    all_gather x1, waiting for transfers between devices, local(): lax.all_gather(tokens, 'tensor', axis=1, tiled=True)  46.5 us
    all_gather x1, waiting for transfers between devices, local(): lax.all_gather(out_grad, 'tensor', axis=1, tiled=True)  40.3 us
  transfers between devices with their start and end apart: 5, of which 5 were waited for; matrix products, arithmetic and copies ran while one was open for 3% of the time, Pallas kernels for 0%

profile of v2, /device:TPU:1, one launch (start us, length us, event | category | flops | bytes accessed | tf_op | source)
XLA Modules:
  0.0 765.4 jit_solution(4234487696986205068)
XLA Ops:
  7.2 1.7 copy.18
  9.0 1.7 copy.15
  10.8 0.7 compare_and_fusion
  11.5 46.5 %all-gather.7.cloned.1.call-done = bf16[256,4096]{0,1:T(8,128)(2,1)} async-done(((bf16[256,256]{0,1:T(8,128)(2,1)}), bf16[256,4096]{0,1:T(8,128)(2,1)}) %all-gather.7.cloned.1.call-update) | async-done | bytes 2097168 | tf_op jit(solution)/shard_map/all_gather | solution.py:14
  58.0 3.2 copy.19
  61.2 40.3 %all-gather.5.cloned.1.call-done = bf16[256,4096]{0,1:T(8,128)(2,1)} async-done(((bf16[256,256]{0,1:T(8,128)(2,1)}), bf16[256,4096]{0,1:T(8,128)(2,1)}) %all-gather.5.cloned.1.call-update) | async-done | bytes 2097168 | tf_op jit(solution)/shard_map/all_gather | solution.py:15
  101.5 4.1 copy.16
  105.6 1.9 gather_fusion.1
  107.5 2.5 gather_fusion
  110.1 0.6 fusion.24
  110.7 0.5 copy-done.2
  111.2 0.8 copy-done.3
  112.0 0.6 fusion.25
  112.7 3.6 multiply_convert_fusion
  116.3 3.7 fusion.20
  120.0 0.1 copy.21
  120.0 0.8 gather_fusion.2
  120.9 2.3 floor_convert_fusion.1
  123.2 1.4 copy.52
  124.7 0.2 reduce-scatter.5.cloned.1.call-start
  125.0 1.9 gather_fusion.3
  126.9 2.8 floor_convert_fusion
  129.7 1.4 copy.51
  131.3 0.6 fusion.26
  131.9 7.7 fusion.6
  139.6 199.7 %reduce-scatter.3.cloned.1.call-done = bf16[24,512]{1,0:T(8,128)(2,1)} async-done(((bf16[24,16384]{1,0:T(8,128)(2,1)}), bf16[24,512]{1,0:T(8,128)(2,1)}) %reduce-scatter.3.cloned.1.call-update) | async-done | bytes 24592 | tf_op jit(solution)/shard_map/reduce_scatter | solution.py:68
  339.3 1.4 convert_multiply_fusion.1
  340.6 221.7 %reduce-scatter.5.cloned.1.call-done = bf16[24,512]{1,0:T(8,128)(2,1)} async-done(((bf16[24,16384]{1,0:T(8,128)(2,1)}), bf16[24,512]{1,0:T(8,128)(2,1)}) %reduce-scatter.5.cloned.1.call-update) | async-done | bytes 24592 | tf_op jit(solution)/shard_map/reduce_scatter | solution.py:71
  562.3 1.4 convert_multiply_fusion
  563.7 181.2 %all-gather.9.cloned.1.call-done = bf16[512,256,128]{2,0,1:T(8,128)(2,1)} async-done(((bf16[32,256,128]{2,0,1:T(8,128)(2,1)}), bf16[512,256,128]{2,0,1:T(8,128)(2,1)}) %all-gather.9.cloned.1.call-update) | async-done | bytes 33554448 | tf_op jit(solution)/shard_map/all_gather | solution.py:49
  744.9 11.6 %reduce_sum.12 = bf16[32,256,128]{2,0,1:T(8,128)(2,1)S(1)} reduce(bf16[16,32,256,128]{3,1,0,2:T(8,128)(2,1)} %bitcast.42, bf16[]{:T(256)} %constant.27.clone.1), dimensions={0}, to_apply=%region_0.0 | reduce | flops 15728640 | bytes 35651584 | tf_op jit(solution)/shard_map/reduce_sum | solution.py:49
  756.6 2.3 copy.50
  (24 shorter events, 0.4 us)
Async XLA Ops:
  7.2 104.0 %copy-start = (bf16[24,128,128]{2,1,0:T(8,128)(2,1)S(1)}, bf16[24,128,128]{2,1,0:T(8,128)(2,1)}, u32[]{:S(2)}) copy-start(bf16[24,128,128]{2,1,0:T(8,128)(2,1)} %param.12) | copy-start | bytes 2359300
  7.2 50.8 %all-gather.7.cloned.1.call-start = ((), (), s32[]{:S(2)}) async-start(), calls=%async_computation.3 | async-start | bytes 2228224 | tf_op jit(solution)/shard_map/all_gather | solution.py:14
  9.0 92.5 %all-gather.5.cloned.1.call-start = ((), (), s32[]{:S(2)}) async-start(), calls=%async_computation.2 | async-start | bytes 2228224 | tf_op jit(solution)/shard_map/all_gather | solution.py:15
  10.7 328.6 %reduce-scatter.3.cloned.1.call-start = ((), (), s32[]{:S(2)}) async-start(), calls=%async_computation.4 | async-start | bytes 811008 | tf_op jit(solution)/shard_map/reduce_scatter | solution.py:68
  107.5 2.5 copy-start.4
  110.0 1.2 copy-start.2
  110.1 2.0 copy-start.3
  124.7 437.6 %reduce-scatter.5.cloned.1.call-start = ((), (), s32[]{:S(2)}) async-start(), calls=%async_computation.5 | async-start | bytes 811008 | tf_op jit(solution)/shard_map/reduce_scatter | solution.py:71
  129.7 1.5 copy-start.5
  131.2 613.7 %all-gather.9.cloned.1.call-start = ((), (), s32[]{:S(2)}) async-start(), calls=%async_computation.6 | async-start | bytes 35651584 | tf_op jit(solution)/shard_map/all_gather | solution.py:49
  756.5 2.3 copy-start.1
Sparse Core Ops, SparseCore 0:
  10.1 47.7 all-gather.6
  60.7 40.7 all-gather.4
  124.8 214.4 reduce-scatter.2
  343.5 218.7 reduce-scatter.4
  564.9 179.9 all-gather.8
